TPU v7x, 512 devices: a whole 4x4x16 slice. The times are simulated.
512 devices in a mesh: rowa: 16 (over y, x), rowb: 32 (over z, core).
Axes of the slice: x: 4, y: 4, z: 16, core: 2. Of those that a mesh axis runs over, the one named last changes fastest.
Arguments:
- right_side: float32 [196608, 8], P(('rowa', 'rowb')), may hold values from -6 to 6
- leaves: float32 [196608, 384], P(('rowa', 'rowb')), as said below
- bases: float32 [9, 196608, 128], P(None, ('rowa', 'rowb')), may hold values from -0.3125 to 0.3125
- ranks: int32 [511], replicated, may hold values from 64 to 128
Outputs:
- solution: float32 [196608, 8], P(('rowa', 'rowb'))
Inputs may be any that keep to these rules, and one draw needn't show every extreme that they name: `ranks`: entry 2^(9 - m) + k - 1 is the rank of node k of level m (levels counted from the leaves, the root at level 9). `leaves`: each leaf block is symmetric positive definite.
All inputs are finite; a program needn't handle non-finite values.
Results may differ from a plain program's by a relative error of at most 0.0001.
Values sent between devices are 32-bit elements; how exact they have to be, the bound alone decides.
A program may use at most 64 MiB of HBM per device.

v0:
```python
import jax
import jax.numpy as jnp
from jax import lax
from jax.experimental import pallas as pl
from jax.experimental.pallas import tpu as pltpu
from jax.sharding import PartitionSpec as P

F32 = jnp.float32
MESH = pl.DeviceIdType.MESH
R = 128
LEAF = 384
LEVELS = 9
NZ, NX, NY = 16, 4, 4
WROWS = LEVELS * R + 16
WUSED = LEVELS * R + 8
HALF = {2: 456, 3: 392}
PART, SUB = 112, 56
ZHALF = NZ * PART
ZROWS = 2 * ZHALF
O4 = 776
O = {5: 1552, 6: 2200, 7: 2720, 8: 3112, 9: 3376}
OEND = 3512
XROWS, YROWS = 1312, 400


def dot(a, b, ca=1, cb=0):
    dims = (((ca,), (cb,)), ((), ()))
    ah, bh = a.astype(jnp.bfloat16), b.astype(jnp.bfloat16)
    al, bl = (a - ah.astype(F32)).astype(jnp.bfloat16), (b - bh.astype(F32)).astype(jnp.bfloat16)

    def times(p, q):
        return lax.dot_general(p, q, dims, preferred_element_type=F32)

    return times(ah, bh) + (times(ah, bl) + times(al, bh))


def wo(level):
    return (level - 1) * R


def rows_of(level):
    return (LEVELS + 1 - level) * R + 8


def strip(a, lo, count, low=0):
    height = a.shape[0]
    lane = lax.broadcasted_iota(jnp.int32, (8, R), 1)
    sub = lax.broadcasted_iota(jnp.int32, (8, R), 0)
    lanes = lax.broadcasted_iota(jnp.int32, (height, R), 1)
    for step in range(0, 8 * count, 8):
        at, first = lo + step, low + step
        panel = a[first : first + 8, :]
        small = [jnp.broadcast_to(panel[:, at + j : at + j + 1], (8, R)) for j in range(8)]
        wide = [jnp.broadcast_to(a[:, at + j : at + j + 1], (height, R)) for j in range(8)]
        rows = jnp.where((lane >= at) & (lane < at + 8), jnp.where(lane - at == sub, 1.0, 0.0), panel)
        for k in range(8):
            pivot = 1.0 / small[k][k : k + 1, :]
            here = sub == k
            column = small[k]
            line = jnp.broadcast_to(rows[k : k + 1, :] * pivot, (8, R))
            rows = jnp.where(here, line, rows - column * line)
            for j in range(k + 1, 8):
                line = jnp.broadcast_to(small[j][k : k + 1, :] * pivot, (8, R))
                small[j] = jnp.where(here, line, small[j] - column * line)
        rest = jnp.where((lanes >= at) & (lanes < at + 8), 0.0, a)
        for j in range(8):
            rest = rest - wide[j] * rows[j : j + 1, :]
        parts = [part for part in (rest[:first], rows, rest[first + 8 :]) if part.shape[0]]
        a = jnp.concatenate(parts, axis=0)
    return a


def inv128(a):
    def step(_, a):
        a = strip(a, 0, 4)
        return pltpu.roll(jnp.concatenate([a[32:], a[:32]], axis=0), R - 32, 1)

    return lax.fori_loop(0, 4, step, a)


def inv_pair(a, b):
    lanes = lax.broadcasted_iota(jnp.int32, (R, R), 1)

    def step(_, pair):
        given = []
        for a in pair:
            rows = strip(a[:32], 0, 4)
            rest = jnp.where(lanes < 32, 0.0, a)[32:] - jnp.dot(
                a[32:, :32], rows, precision=lax.Precision.HIGHEST, preferred_element_type=F32
            )
            given.append(pltpu.roll(jnp.concatenate([rest, rows], axis=0), R - 32, 1))
        return tuple(given)

    return lax.fori_loop(0, 4, step, (a, b))


def eye():
    row = lax.broadcasted_iota(jnp.int32, (R, R), 0)
    column = lax.broadcasted_iota(jnp.int32, (R, R), 1)
    return jnp.where(row == column, 1.0, 0.0).astype(F32)


def flipped(value, mask):
    for bit in (1, 2, 4, 8):
        if mask & bit:
            value = value + bit - 2 * bit * ((value // bit) % 2)
    return value


def kernel(
    ranks, rhs, leaves, bases, out,
    zz, wt, dd, pt, r1, a2, b2, t2, s2, a3, b3, c3, s3, s3b, t3,
    bb, rz, hh, s_r, r_r, s_l, r_l, tt, xm, xb, u6, s7, ym, yb,
    send_sems, recv_sems,
):
    ra, rb = lax.axis_index("rowa"), lax.axis_index("rowb")
    y, x, z, c = ra // NX, ra % NX, rb // 2, rb % 2
    position = ra * (2 * NZ) + rb

    def device(y=y, x=x, z=z, c=c):
        return (y * NX + x, z * 2 + c)

    partner = device(c=1 - c)
    above, below = device(z=(z + 1) % NZ), device(z=(z + NZ - 1) % NZ)
    z1, z2 = device(z=flipped(z, 1)), device(z=flipped(z, 2))
    xs = [device(x=flipped(x, i)) for i in (1, 2, 3)]
    ys = [device(y=flipped(y, i)) for i in (1, 2, 3)]
    met = [partner, above, below, z2] + xs + ys
    barrier = pltpu.get_barrier_semaphore()
    for other in met:
        pl.semaphore_signal(barrier, inc=1, device_id=other, device_id_type=MESH)

    used = [0]
    started = []

    def send(src, dst, to):
        at = used[0]
        used[0] += 1
        copy = pltpu.make_async_remote_copy(
            src_ref=src, dst_ref=dst, send_sem=send_sems.at[at], recv_sem=recv_sems.at[at],
            device_id=to, device_id_type=MESH,
        )
        copy.start()
        started.append(copy)
        return copy

    def sent():
        for copy in started:
            copy.wait_send()
        started.clear()

    dd[...] = leaves[...]

    @pl.loop(0, 3)
    def _(_k):
        inverse = inv128(dd[:R, :R])
        line = dot(inverse, dd[:R, R:])
        column = dd[R:, :R]
        inner = dd[R:, R:] - dot(column, line)
        edge = dot(column, inverse)
        dd[: 2 * R, : 2 * R] = inner
        dd[: 2 * R, 2 * R :] = -edge
        dd[2 * R :, : 2 * R] = line
        dd[2 * R :, 2 * R :] = inverse

    lane = lax.broadcasted_iota(jnp.int32, (LEAF, R), 1)
    for level in range(1, LEVELS + 1):
        rank = ranks[2 ** (LEVELS - level) + position // 2**level - 1]
        zz[level - 1] = jnp.where(lane < rank, bases[level - 1], 0.0)

    @pl.loop(0, LEVELS)
    def _(j):
        wt[pl.ds(pl.multiple_of(j * R, R), R), :] = dot(zz[j], dd[...], 0, 0)

    wt[pl.ds(LEVELS * R, 8), :] = dot(rhs[...], dd[...])
    wt[pl.ds(WUSED, 8), :] = jnp.zeros((8, LEAF), F32)

    pl.semaphore_wait(barrier, len(met))

    def head(level):
        pt[level - 1, :R, :] = dot(wt[pl.ds(wo(level), R), :], zz[level - 1])

    def tail(level):
        count = WROWS - wo(level) - R
        pt[level - 1, pl.ds(R, count), :] = dot(wt[pl.ds(wo(level) + R, count), :], zz[level - 1])

    def eliminated(mine, total, level, between):
        first = pl.ds(wo(level + 1), R)
        wt[first, :] = wt[first, :] - dot(total[pl.ds(R, R), :], mine)
        between()
        count = WROWS - wo(level + 2)
        rest = pl.ds(wo(level + 2), count)
        wt[rest, :] = wt[rest, :] - dot(total[pl.ds(2 * R, count), :], mine)

    def pulled(inverse, level):
        return dot(inverse, wt[pl.ds(wo(level), R), :])

    count = WROWS - R
    head(1)
    ahead = send(pt.at[0, pl.ds(0, R), :], r1.at[pl.ds(0, R), :], partner)
    tail(1)
    later = send(pt.at[0, pl.ds(R, count), :], r1.at[pl.ds(R, count), :], partner)
    ahead.wait_recv()
    mine = pulled(inv128(eye() + (r1[:R, :] + pt[0, :R, :])), 1)
    later.wait_recv()
    r1[R:, :] = r1[R:, :] + pt[0, pl.ds(R, count), :]

    def spans(level):
        half = HALF[level]
        far = 1 - c
        return (
            (pl.ds(0, 64), pl.ds(pl.multiple_of(c * 64, 8), 64), pl.ds(pl.multiple_of(far * 64, 8), 64)),
            (
                pl.ds(64, half),
                pl.ds(pl.multiple_of(R + c * half, 8), half),
                pl.ds(pl.multiple_of(R + far * half, 8), half),
            ),
        )

    copies = []

    def lead(level, near):
        def run():
            head(level)
            where, _, far = spans(level)[0]
            copies.append(send(pt.at[level - 1, far, :], near.at[where, :], partner))

        return run

    def follow(level, near):
        tail(level)
        where, _, far = spans(level)[1]
        copies.append(send(pt.at[level - 1, far, :], near.at[where, :], partner))

    eliminated(mine, r1, 1, lead(2, a2))
    follow(2, a2)
    crossing = []
    for (where, own, _), copy in zip(spans(2), copies):
        copy.wait_recv()
        s2[where, :] = pt[1, own, :] + a2[where, :]
        crossing.append(send(s2.at[where, :], b2.at[where, :], z1))
    copies.clear()
    for part_of, ((where, own, _), copy) in enumerate(zip(spans(2), crossing)):
        copy.wait_recv()
        t2[own, :] = s2[where, :] + b2[where, :]
        last = send(t2.at[own, :], t2.at[own, :], partner)
        last.wait_recv()
        if part_of == 0:
            mine = pulled(inv128(eye() + t2[:R, :]), 2)

    eliminated(mine, t2, 2, lead(3, a3))
    follow(3, a3)
    crossing = []
    for (where, own, _), copy in zip(spans(3), copies):
        copy.wait_recv()
        s3[where, :] = pt[2, own, :] + a3[where, :]
        crossing.append(send(s3.at[where, :], b3.at[where, :], z1))
    farther = []
    for (where, own, _), copy in zip(spans(3), crossing):
        copy.wait_recv()
        s3b[where, :] = s3[where, :] + b3[where, :]
        farther.append(send(s3b.at[where, :], c3.at[where, :], z2))
    for part_of, ((where, own, _), copy) in enumerate(zip(spans(3), farther)):
        copy.wait_recv()
        t3[own, :] = s3b[where, :] + c3[where, :]
        last = send(t3.at[own, :], t3.at[own, :], partner)
        last.wait_recv()
        if part_of == 0:
            mine = pulled(inv128(eye() + t3[:R, :]), 3)
    eliminated(mine, t3, 3, lambda: None)

    side = z // 8
    mine4 = pl.multiple_of(side * O4, 8)
    bb[pl.ds(mine4, O4), :] = dot(wt[pl.ds(wo(4), O4), :], zz[3])
    bb[pl.ds(pl.multiple_of((1 - side) * O4, 8), O4), :] = jnp.zeros((O4, R), F32)
    for level in range(5, LEVELS + 1):
        n = rows_of(level)
        bb[pl.ds(O[level], n), :] = dot(wt[pl.ds(wo(level), n), :], zz[level - 1])
    bb[pl.ds(OEND, ZROWS - OEND), :] = jnp.zeros((ZROWS - OEND, R), F32)

    own = c * ZHALF
    other = (1 - c) * ZHALF

    def part(of, u=0, rows=PART, base=0):
        return pl.ds(pl.multiple_of(base + of * PART + u * SUB, 8), rows)

    order = [(z + 7) % NZ, (z + 8) % NZ]
    for s in range(1, 8):
        order += [(z + 7 - s) % NZ, (z + 8 + s) % NZ]
    gathered = [send(bb.at[part(of, 0, PART, other), :], rz.at[part(of), :], partner) for of in order]

    def summed(at):
        gathered[at].wait_recv()
        here = part(order[at])
        hh[here, :] = bb[part(order[at], 0, PART, own), :] + rz[here, :]

    right, left = [None, None], [None, None]
    for s in range(8):
        if s < 7:
            summed(2 * s)
        summed(2 * s + 1 if s < 7 else 15)
        for u in range(2):
            rows = pl.ds(u * SUB, SUB)
            if s < 7:
                to = part((z + 7 - s) % NZ, u, SUB)
                source = hh.at[to, :]
                if s > 0:
                    right[u].wait_recv()
                    s_r[s - 1, rows, :] = hh[to, :] + r_r[s - 1, rows, :]
                    source = s_r.at[s - 1, rows, :]
                right[u] = send(source, r_r.at[s, rows, :], above)
            to = part((z + 8 + s) % NZ, u, SUB)
            source = hh.at[to, :]
            if s > 0:
                left[u].wait_recv()
                s_l[s - 1, rows, :] = hh[to, :] + r_l[s - 1, rows, :]
                source = s_l.at[s - 1, rows, :]
            left[u] = send(source, r_l.at[s, rows, :], below)
    summed(14)
    across = []
    from_left, from_right = [None, None], [None, None]

    def place(of, u):
        return part(of % NZ, u, SUB, own)

    for u in range(2):
        rows = pl.ds(u * SUB, SUB)
        right[u].wait_recv()
        left[u].wait_recv()
        here = place(z, u)
        tt[here, :] = hh[part(z, u, SUB), :] + r_r[6, rows, :] + r_l[7, rows, :]
        from_left[u] = send(tt.at[here, :], tt.at[here, :], above)
        from_right[u] = send(tt.at[here, :], tt.at[here, :], below)
        across.append(send(tt.at[here, :], tt.at[here, :], partner))
    for s in range(1, 9):
        for u in range(2):
            from_left[u].wait_recv()
            here = place(z + NZ - s, u)
            if s < 8:
                from_left[u] = send(tt.at[here, :], tt.at[here, :], above)
            across.append(send(tt.at[here, :], tt.at[here, :], partner))
            if s < 8:
                from_right[u].wait_recv()
                here = place(z + s, u)
                if s < 7:
                    from_right[u] = send(tt.at[here, :], tt.at[here, :], below)
                across.append(send(tt.at[here, :], tt.at[here, :], partner))
    for copy in across:
        copy.wait_recv()
    sent()

    both4 = inv_pair(eye() + tt[pl.ds(0, R), :], eye() + tt[pl.ds(O4, R), :])
    halves = [dot(tt[pl.ds(k * O4 + R, O4 - R), :], both4[k]) for k in range(2)]
    for level in range(5, LEVELS + 1):
        n = rows_of(level)
        skip = wo(level) - wo(5)
        there = pl.ds(O[level], n)
        value = tt[there, :]
        for k in range(2):
            value = value - dot(halves[k][skip:], tt[pl.ds(k * O4 + R + skip, R), :], 1, 1)
        tt[there, :] = value

    inverse5 = inv128(eye() + tt[pl.ds(O[5], R), :])
    rest5 = tt[pl.ds(O[5] + R, rows_of(6)), :]
    half5 = dot(rest5, inverse5)
    for level in range(6, LEVELS + 1):
        n = rows_of(level)
        skip = wo(level) - wo(6)
        xm[pl.ds(O[level] - O[6], n), :] = tt[pl.ds(O[level], n), :] - dot(
            half5[skip:], rest5[skip : skip + R], 1, 1
        )

    def exchanged(block, slots, rows, others, meanwhile):
        half = (rows - R) // 2
        kept = []
        for start, span in ((0, 64), (R, half)):
            lines = pl.ds(pl.multiple_of(start + c * span, 8), span)
            kept.append((lines, [send(block.at[lines, :], slots.at[i, lines, :], others[i]) for i in range(3)]))
        given = None
        for lines, first in kept:
            second = []
            for i in (0, 2, 1):
                first[i].wait_recv()
                second.append(send(slots.at[i, lines, :], slots.at[i, lines, :], partner))
            for copy in second:
                copy.wait_recv()
            if given is None:
                given = meanwhile()
        return given

    def update45():
        mine = dot(jnp.where(side == 0, both4[0], both4[1]), wt[pl.ds(wo(4), R), :])
        rest = pl.ds(wo(5), WUSED - wo(5))
        wt[rest, :] = wt[rest, :] - dot(
            tt[pl.ds(pl.multiple_of(mine4 + R, 8), O4 - R), :], mine
        )
        mine = dot(inverse5, wt[pl.ds(wo(5), R), :])
        rest = pl.ds(wo(6), WUSED - wo(6))
        wt[rest, :] = wt[rest, :] - dot(rest5, mine)

    def inverses6():
        lines = pl.ds(0, R)
        pair = inv_pair(
            eye() + (xm[lines, :] + xb[0, lines, :]), eye() + (xb[1, lines, :] + xb[2, lines, :])
        )
        update45()
        return pair

    both6 = exchanged(xm, xb, XROWS, xs, inverses6)
    u6[0] = xm[pl.ds(0, 520), :] + xb[0, pl.ds(0, 520), :]
    u6[1] = xb[1, pl.ds(0, 520), :] + xb[2, pl.ds(0, 520), :]
    halves = [dot(u6[k, pl.ds(R, 392), :], both6[k]) for k in range(2)]
    for level in range(7, LEVELS + 1):
        n = rows_of(level)
        skip = wo(level) - wo(7)
        there = pl.ds(O[level] - O[6], n)
        value = (xm[there, :] + xb[0, there, :]) + (xb[1, there, :] + xb[2, there, :])
        for k in range(2):
            value = value - dot(halves[k][skip:], u6[k, pl.ds(R + skip, R), :], 1, 1)
        s7[pl.ds(O[level] - O[7], n), :] = value
    inverse7 = inv128(eye() + s7[pl.ds(0, R), :])
    rest7 = s7[pl.ds(R, 264), :]
    half7 = dot(rest7, inverse7)
    ym[pl.ds(0, 264), :] = s7[pl.ds(392, 264), :] - dot(half7, rest7[:R], 1, 1)
    ym[pl.ds(264, 136), :] = s7[pl.ds(656, 136), :] - dot(half7[R:], rest7[R : 2 * R], 1, 1)

    def inverses8():
        lines = pl.ds(0, R)
        return inv_pair(
            eye() + (ym[lines, :] + yb[0, lines, :]), eye() + (yb[1, lines, :] + yb[2, lines, :])
        )

    inverses = exchanged(ym, yb, YROWS, ys, inverses8)
    top = pl.ds(0, 264)
    u8 = [ym[top, :] + yb[0, top, :], yb[1, top, :] + yb[2, top, :]]
    there = pl.ds(264, 136)
    s9 = (ym[there, :] + yb[0, there, :]) + (yb[1, there, :] + yb[2, there, :])
    for k in range(2):
        rest = u8[k][R:]
        s9 = s9 - dot(dot(rest, inverses[k]), rest[:R], 1, 1)
    inverse9 = inv128(eye() + s9[:R])

    x9 = dot(s9[R:], inverse9)
    x8 = dot(u8[0][2 * R :] - dot(x9, u8[0][R : 2 * R]), inverses[0])
    right7 = s7[pl.ds(384, 8), :] - dot(x9, s7[pl.ds(256, R), :]) - dot(x8, s7[pl.ds(128, R), :])
    x7 = dot(right7, inverse7)
    right6 = u6[0, pl.ds(512, 8), :] - dot(x9, u6[0, pl.ds(384, R), :])
    right6 = right6 - dot(x8, u6[0, pl.ds(256, R), :]) - dot(x7, u6[0, pl.ds(128, R), :])
    x6 = dot(right6, both6[0])
    found = wt[pl.ds(LEVELS * R, 8), :]
    for level, value in ((9, x9), (8, x8), (7, x7), (6, x6)):
        found = found - dot(value, wt[pl.ds(wo(level), R), :])
    out[...] = found
    sent()


def body(right_side, leaves, bases, ranks):
    v = lambda *shape: pltpu.VMEM(shape, F32)
    vmem = pl.BlockSpec(memory_space=pltpu.VMEM)
    near2, near3 = 64 + HALF[2], 64 + HALF[3]
    scratch = [
        v(LEVELS, LEAF, R), v(WROWS, LEAF), v(LEAF, LEAF), v(3, WROWS, R), v(WROWS, R),
        v(near2, R), v(near2, R), v(2 * near2, R), v(near2, R),
        v(near3, R), v(near3, R), v(near3, R), v(near3, R), v(near3, R), v(2 * near3, R),
        v(ZROWS, R), v(ZHALF, R), v(ZHALF, R), v(6, PART, R), v(7, PART, R), v(7, PART, R), v(8, PART, R),
        v(ZROWS, R), v(XROWS, R), v(3, XROWS, R), v(2, 520, R), v(792, R),
        v(YROWS, R), v(3, YROWS, R),
        pltpu.SemaphoreType.DMA((160,)), pltpu.SemaphoreType.DMA((160,)),
    ]
    return pl.pallas_call(
        kernel,
        out_shape=jax.ShapeDtypeStruct((8, LEAF), F32),
        in_specs=[pl.BlockSpec(memory_space=pltpu.SMEM), vmem, vmem, vmem],
        out_specs=vmem,
        scratch_shapes=scratch,
        compiler_params=pltpu.CompilerParams(
            collective_id=0, has_side_effects=True, vmem_limit_bytes=60 * 2**20
        ),
        name="tree",
    )(ranks, right_side.T, leaves, bases).T


def solution(mesh):
    rows = P(("rowa", "rowb"), None)
    return jax.shard_map(
        body, mesh=mesh, in_specs=(rows, rows, P(None, ("rowa", "rowb"), None), P()),
        out_specs=rows, check_vma=False,
    )
```

profile of v0, /device:TPU:1, one launch (start us, length us, event | category | flops | bytes accessed | tf_op | source)
XLA Modules:
  0.0 187.2 jit_solution(4069505016330260850)
XLA Ops:
  0.0 185.8 %tree.1 = f32[8,384]{1,0:T(8,128)} custom-call(s32[511]{0:T(512)} %ranks.1, f32[8,384]{1,0:T(8,128)} %bitcast.3, f32[384,384]{1,0:T(8,128)} %leaves.1, f32[9,384,128]{2,1,0:T(8,128)} %bases.1), custom_call_target="tpu_custom_call" | custom-call | tf_op jit(solution)/shard_map/tree/pallas_call | solution.py:470
  185.9 1.3 copy.6
where the time goes:
time: 187 us
  Pallas kernels  186 us (99%)
    pallas_call x1, Pallas kernels, body(): pl.pallas_call(kernel, out_shape=jax.ShapeDtypeStruct((8, LEAF), F32), in...  186 us

commit v1 on v0

--- a/solution.py
+++ b/solution.py
@@ -78,6 +78,10 @@
     return lax.fori_loop(0, 4, step, a)
 
 
+def inv_flat(a):
+    return strip(a, 0, 16)
+
+
 def inv_pair(a, b):
     lanes = lax.broadcasted_iota(jnp.int32, (R, R), 1)
 
@@ -123,8 +127,8 @@
     partner = device(c=1 - c)
     above, below = device(z=(z + 1) % NZ), device(z=(z + NZ - 1) % NZ)
     z1, z2 = device(z=flipped(z, 1)), device(z=flipped(z, 2))
-    xs = [device(x=flipped(x, i)) for i in (1, 2, 3)]
-    ys = [device(y=flipped(y, i)) for i in (1, 2, 3)]
+    xs = [device(x=(x + 1) % NX), device(x=(x + NX - 1) % NX)]
+    ys = [device(y=(y + 1) % NY), device(y=(y + NY - 1) % NY)]
     met = [partner, above, below, z2] + xs + ys
     barrier = pltpu.get_barrier_semaphore()
     for other in met:
@@ -153,7 +157,7 @@
 
     @pl.loop(0, 3)
     def _(_k):
-        inverse = inv128(dd[:R, :R])
+        inverse = inv_flat(dd[:R, :R])
         line = dot(inverse, dd[:R, R:])
         column = dd[R:, :R]
         inner = dd[R:, R:] - dot(column, line)
@@ -168,13 +172,7 @@
         rank = ranks[2 ** (LEVELS - level) + position // 2**level - 1]
         zz[level - 1] = jnp.where(lane < rank, bases[level - 1], 0.0)
 
-    @pl.loop(0, LEVELS)
-    def _(j):
-        wt[pl.ds(pl.multiple_of(j * R, R), R), :] = dot(zz[j], dd[...], 0, 0)
-
-    wt[pl.ds(LEVELS * R, 8), :] = dot(rhs[...], dd[...])
-    wt[pl.ds(WUSED, 8), :] = jnp.zeros((8, LEAF), F32)
-
+    wt[:R, :] = dot(zz[0], dd[...], 0, 0)
     pl.semaphore_wait(barrier, len(met))
 
     def head(level):
@@ -198,6 +196,13 @@
     count = WROWS - R
     head(1)
     ahead = send(pt.at[0, pl.ds(0, R), :], r1.at[pl.ds(0, R), :], partner)
+
+    @pl.loop(1, LEVELS)
+    def _(j):
+        wt[pl.ds(pl.multiple_of(j * R, R), R), :] = dot(zz[j], dd[...], 0, 0)
+
+    wt[pl.ds(LEVELS * R, 8), :] = dot(rhs[...], dd[...])
+    wt[pl.ds(WUSED, 8), :] = jnp.zeros((8, LEAF), F32)
     tail(1)
     later = send(pt.at[0, pl.ds(R, count), :], r1.at[pl.ds(R, count), :], partner)
     ahead.wait_recv()
@@ -360,33 +365,53 @@
             value = value - dot(halves[k][skip:], tt[pl.ds(k * O4 + R + skip, R), :], 1, 1)
         tt[there, :] = value
 
-    inverse5 = inv128(eye() + tt[pl.ds(O[5], R), :])
+    inverse5 = inv_flat(eye() + tt[pl.ds(O[5], R), :])
     rest5 = tt[pl.ds(O[5] + R, rows_of(6)), :]
-    half5 = dot(rest5, inverse5)
-    for level in range(6, LEVELS + 1):
-        n = rows_of(level)
-        skip = wo(level) - wo(6)
-        xm[pl.ds(O[level] - O[6], n), :] = tt[pl.ds(O[level], n), :] - dot(
-            half5[skip:], rest5[skip : skip + R], 1, 1
-        )
-
-    def exchanged(block, slots, rows, others, meanwhile):
+    xm[:R, :] = tt[pl.ds(O[6], R), :] - dot(dot(rest5[:R], inverse5), rest5[:R], 1, 1)
+
+    def prepared5():
+        half5 = dot(rest5, inverse5)
+        for level in range(6, LEVELS + 1):
+            skip = wo(level) - wo(6)
+            first = R if level == 6 else 0
+            n = rows_of(level) - first
+            xm[pl.ds(O[level] - O[6] + first, n), :] = tt[pl.ds(O[level] + first, n), :] - dot(
+                half5[skip + first :], rest5[skip : skip + R], 1, 1
+            )
+
+    def exchanged(block, slots, rows, others, prepare, invert, fill):
+        after, before = others
         half = (rows - R) // 2
-        kept = []
-        for start, span in ((0, 64), (R, half)):
-            lines = pl.ds(pl.multiple_of(start + c * span, 8), span)
-            kept.append((lines, [send(block.at[lines, :], slots.at[i, lines, :], others[i]) for i in range(3)]))
-        given = None
-        for lines, first in kept:
-            second = []
-            for i in (0, 2, 1):
-                first[i].wait_recv()
-                second.append(send(slots.at[i, lines, :], slots.at[i, lines, :], partner))
-            for copy in second:
+        cut = (half // 16) * 8
+        streams = []
+        for start, span, piece in ((0, 64, 32), (R, half, cut)):
+            base = start + c * span
+            lines = pl.ds(pl.multiple_of(base, 8), span)
+            one = pl.ds(pl.multiple_of(base, 8), piece)
+            two = pl.ds(pl.multiple_of(base + piece, 8), span - piece)
+            up = send(block.at[lines, :], slots.at[0, lines, :], after)
+            down = send(block.at[lines, :], slots.at[1, lines, :], before)
+            streams.append((lines, one, two, up, down))
+            if start == 0:
+                prepare()
+        inverses = None
+        for lines, one, two, up, down in streams:
+            up.wait_recv()
+            on = [send(slots.at[0, one, :], slots.at[2, one, :], after)]
+            shared = [send(slots.at[0, lines, :], slots.at[0, lines, :], partner)]
+            down.wait_recv()
+            on.append(send(slots.at[1, two, :], slots.at[2, two, :], before))
+            shared.append(send(slots.at[1, lines, :], slots.at[1, lines, :], partner))
+            if inverses is not None:
+                fill()
+            for copy, where in zip(on, (one, two)):
                 copy.wait_recv()
-            if given is None:
-                given = meanwhile()
-        return given
+                shared.append(send(slots.at[2, where, :], slots.at[2, where, :], partner))
+            for copy in shared:
+                copy.wait_recv()
+            if inverses is None:
+                inverses = invert()
+        return inverses
 
     def update45():
         mine = dot(jnp.where(side == 0, both4[0], both4[1]), wt[pl.ds(wo(4), R), :])
@@ -398,47 +423,54 @@
         rest = pl.ds(wo(6), WUSED - wo(6))
         wt[rest, :] = wt[rest, :] - dot(rest5, mine)
 
+    xmate, xnear = 1 - x % 2, x % 2
+
     def inverses6():
         lines = pl.ds(0, R)
-        pair = inv_pair(
-            eye() + (xm[lines, :] + xb[0, lines, :]), eye() + (xb[1, lines, :] + xb[2, lines, :])
+        return inv_pair(
+            eye() + (xm[lines, :] + xb[xmate, lines, :]), eye() + (xb[xnear, lines, :] + xb[2, lines, :])
         )
-        update45()
-        return pair
-
-    both6 = exchanged(xm, xb, XROWS, xs, inverses6)
-    u6[0] = xm[pl.ds(0, 520), :] + xb[0, pl.ds(0, 520), :]
-    u6[1] = xb[1, pl.ds(0, 520), :] + xb[2, pl.ds(0, 520), :]
+
+    both6 = exchanged(xm, xb, XROWS, xs, prepared5, inverses6, update45)
+    u6[0] = xm[pl.ds(0, 520), :] + xb[xmate, pl.ds(0, 520), :]
+    u6[1] = xb[xnear, pl.ds(0, 520), :] + xb[2, pl.ds(0, 520), :]
     halves = [dot(u6[k, pl.ds(R, 392), :], both6[k]) for k in range(2)]
     for level in range(7, LEVELS + 1):
         n = rows_of(level)
         skip = wo(level) - wo(7)
         there = pl.ds(O[level] - O[6], n)
-        value = (xm[there, :] + xb[0, there, :]) + (xb[1, there, :] + xb[2, there, :])
+        value = (xm[there, :] + xb[xmate, there, :]) + (xb[xnear, there, :] + xb[2, there, :])
         for k in range(2):
             value = value - dot(halves[k][skip:], u6[k, pl.ds(R + skip, R), :], 1, 1)
         s7[pl.ds(O[level] - O[7], n), :] = value
-    inverse7 = inv128(eye() + s7[pl.ds(0, R), :])
+    inverse7 = inv_flat(eye() + s7[pl.ds(0, R), :])
     rest7 = s7[pl.ds(R, 264), :]
-    half7 = dot(rest7, inverse7)
-    ym[pl.ds(0, 264), :] = s7[pl.ds(392, 264), :] - dot(half7, rest7[:R], 1, 1)
-    ym[pl.ds(264, 136), :] = s7[pl.ds(656, 136), :] - dot(half7[R:], rest7[R : 2 * R], 1, 1)
+    half7 = dot(rest7[:R], inverse7)
+    ym[:R, :] = s7[pl.ds(392, R), :] - dot(half7, rest7[:R], 1, 1)
+
+    def prepared7():
+        half7 = dot(rest7[R:], inverse7)
+        ym[pl.ds(R, 136), :] = s7[pl.ds(392 + R, 136), :] - dot(half7, rest7[:R], 1, 1)
+        ym[pl.ds(264, 136), :] = s7[pl.ds(656, 136), :] - dot(half7, rest7[R : 2 * R], 1, 1)
+
+
+    ymate, ynear = 1 - y % 2, y % 2
 
     def inverses8():
         lines = pl.ds(0, R)
         return inv_pair(
-            eye() + (ym[lines, :] + yb[0, lines, :]), eye() + (yb[1, lines, :] + yb[2, lines, :])
+            eye() + (ym[lines, :] + yb[ymate, lines, :]), eye() + (yb[ynear, lines, :] + yb[2, lines, :])
         )
 
-    inverses = exchanged(ym, yb, YROWS, ys, inverses8)
+    inverses = exchanged(ym, yb, YROWS, ys, prepared7, inverses8, lambda: None)
     top = pl.ds(0, 264)
-    u8 = [ym[top, :] + yb[0, top, :], yb[1, top, :] + yb[2, top, :]]
+    u8 = [ym[top, :] + yb[ymate, top, :], yb[ynear, top, :] + yb[2, top, :]]
     there = pl.ds(264, 136)
-    s9 = (ym[there, :] + yb[0, there, :]) + (yb[1, there, :] + yb[2, there, :])
+    s9 = (ym[there, :] + yb[ymate, there, :]) + (yb[ynear, there, :] + yb[2, there, :])
     for k in range(2):
         rest = u8[k][R:]
         s9 = s9 - dot(dot(rest, inverses[k]), rest[:R], 1, 1)
-    inverse9 = inv128(eye() + s9[:R])
+    inverse9 = inv_flat(eye() + s9[:R])
 
     x9 = dot(s9[R:], inverse9)
     x8 = dot(u8[0][2 * R :] - dot(x9, u8[0][R : 2 * R]), inverses[0])

time: 187 us -> 192 us (1.027)
  Pallas kernels: 186 us -> 190 us
    pallas_call x1, Pallas kernels: 186 us -> 190 us  [body(): pl.pallas_call(kernel, out_shape=jax.ShapeDtypeStruct((8, LEAF), F32), in...]
where the time goes in v1:
time: 192 us
  Pallas kernels  190 us (99%)
    pallas_call x1, Pallas kernels, body(): pl.pallas_call(kernel, out_shape=jax.ShapeDtypeStruct((8, LEAF), F32), in...  190 us

profile of v1, /device:TPU:1, one launch (start us, length us, event | category | flops | bytes accessed | tf_op | source)
XLA Modules:
  0.0 191.6 jit_solution(6463756098040230994)
XLA Ops:
  0.0 190.3 %tree.1 = f32[8,384]{1,0:T(8,128)} custom-call(s32[511]{0:T(512)} %ranks.1, f32[8,384]{1,0:T(8,128)} %bitcast.3, f32[384,384]{1,0:T(8,128)} %leaves.1, f32[9,384,128]{2,1,0:T(8,128)} %bases.1), custom_call_target="tpu_custom_call" | custom-call | tf_op jit(solution)/shard_map/tree/pallas_call | solution.py:502
  190.3 1.3 copy.6

commit v2 on v1

--- a/solution.py
+++ b/solution.py
@@ -127,8 +127,8 @@
     partner = device(c=1 - c)
     above, below = device(z=(z + 1) % NZ), device(z=(z + NZ - 1) % NZ)
     z1, z2 = device(z=flipped(z, 1)), device(z=flipped(z, 2))
-    xs = [device(x=(x + 1) % NX), device(x=(x + NX - 1) % NX)]
-    ys = [device(y=(y + 1) % NY), device(y=(y + NY - 1) % NY)]
+    xs = [device(x=flipped(x, i)) for i in (1, 2, 3)]
+    ys = [device(y=flipped(y, i)) for i in (1, 2, 3)]
     met = [partner, above, below, z2] + xs + ys
     barrier = pltpu.get_barrier_semaphore()
     for other in met:
@@ -206,21 +206,21 @@
     tail(1)
     later = send(pt.at[0, pl.ds(R, count), :], r1.at[pl.ds(R, count), :], partner)
     ahead.wait_recv()
-    mine = pulled(inv128(eye() + (r1[:R, :] + pt[0, :R, :])), 1)
+    mine = pulled(inv_flat(eye() + (r1[:R, :] + pt[0, :R, :])), 1)
     later.wait_recv()
     r1[R:, :] = r1[R:, :] + pt[0, pl.ds(R, count), :]
 
     def spans(level):
         half = HALF[level]
+        first = (half // 16) * 8 + 8
         far = 1 - c
-        return (
-            (pl.ds(0, 64), pl.ds(pl.multiple_of(c * 64, 8), 64), pl.ds(pl.multiple_of(far * 64, 8), 64)),
-            (
-                pl.ds(64, half),
-                pl.ds(pl.multiple_of(R + c * half, 8), half),
-                pl.ds(pl.multiple_of(R + far * half, 8), half),
-            ),
-        )
+        given = []
+        for near, start, stride, rows in (
+            (0, 0, 64, 64), (64, R, half, first), (64 + first, R + first, half, half - first)
+        ):
+            own = pl.ds(pl.multiple_of(start + c * stride, 8), rows)
+            given.append((pl.ds(near, rows), own, pl.ds(pl.multiple_of(start + far * stride, 8), rows)))
+        return given
 
     copies = []
 
@@ -234,8 +234,8 @@
 
     def follow(level, near):
         tail(level)
-        where, _, far = spans(level)[1]
-        copies.append(send(pt.at[level - 1, far, :], near.at[where, :], partner))
+        for where, _, far in spans(level)[1:]:
+            copies.append(send(pt.at[level - 1, far, :], near.at[where, :], partner))
 
     eliminated(mine, r1, 1, lead(2, a2))
     follow(2, a2)
@@ -245,13 +245,16 @@
         s2[where, :] = pt[1, own, :] + a2[where, :]
         crossing.append(send(s2.at[where, :], b2.at[where, :], z1))
     copies.clear()
+    last = []
     for part_of, ((where, own, _), copy) in enumerate(zip(spans(2), crossing)):
         copy.wait_recv()
         t2[own, :] = s2[where, :] + b2[where, :]
-        last = send(t2.at[own, :], t2.at[own, :], partner)
-        last.wait_recv()
+        last.append(send(t2.at[own, :], t2.at[own, :], partner))
         if part_of == 0:
+            last.pop().wait_recv()
             mine = pulled(inv128(eye() + t2[:R, :]), 2)
+    for copy in last:
+        copy.wait_recv()
 
     eliminated(mine, t2, 2, lead(3, a3))
     follow(3, a3)
@@ -265,13 +268,16 @@
         copy.wait_recv()
         s3b[where, :] = s3[where, :] + b3[where, :]
         farther.append(send(s3b.at[where, :], c3.at[where, :], z2))
+    last = []
     for part_of, ((where, own, _), copy) in enumerate(zip(spans(3), farther)):
         copy.wait_recv()
         t3[own, :] = s3b[where, :] + c3[where, :]
-        last = send(t3.at[own, :], t3.at[own, :], partner)
-        last.wait_recv()
+        last.append(send(t3.at[own, :], t3.at[own, :], partner))
         if part_of == 0:
+            last.pop().wait_recv()
             mine = pulled(inv128(eye() + t3[:R, :]), 3)
+    for copy in last:
+        copy.wait_recv()
     eliminated(mine, t3, 3, lambda: None)
 
     side = z // 8
@@ -380,33 +386,21 @@
             )
 
     def exchanged(block, slots, rows, others, prepare, invert, fill):
-        after, before = others
         half = (rows - R) // 2
-        cut = (half // 16) * 8
         streams = []
-        for start, span, piece in ((0, 64, 32), (R, half, cut)):
-            base = start + c * span
-            lines = pl.ds(pl.multiple_of(base, 8), span)
-            one = pl.ds(pl.multiple_of(base, 8), piece)
-            two = pl.ds(pl.multiple_of(base + piece, 8), span - piece)
-            up = send(block.at[lines, :], slots.at[0, lines, :], after)
-            down = send(block.at[lines, :], slots.at[1, lines, :], before)
-            streams.append((lines, one, two, up, down))
+        for start, span in ((0, 64), (R, half)):
+            lines = pl.ds(pl.multiple_of(start + c * span, 8), span)
+            streams.append((lines, [send(block.at[lines, :], slots.at[i, lines, :], others[i]) for i in range(3)]))
             if start == 0:
                 prepare()
         inverses = None
-        for lines, one, two, up, down in streams:
-            up.wait_recv()
-            on = [send(slots.at[0, one, :], slots.at[2, one, :], after)]
-            shared = [send(slots.at[0, lines, :], slots.at[0, lines, :], partner)]
-            down.wait_recv()
-            on.append(send(slots.at[1, two, :], slots.at[2, two, :], before))
-            shared.append(send(slots.at[1, lines, :], slots.at[1, lines, :], partner))
+        for lines, first in streams:
             if inverses is not None:
                 fill()
-            for copy, where in zip(on, (one, two)):
-                copy.wait_recv()
-                shared.append(send(slots.at[2, where, :], slots.at[2, where, :], partner))
+            shared = []
+            for i in (0, 2, 1):
+                first[i].wait_recv()
+                shared.append(send(slots.at[i, lines, :], slots.at[i, lines, :], partner))
             for copy in shared:
                 copy.wait_recv()
             if inverses is None:
@@ -423,23 +417,21 @@
         rest = pl.ds(wo(6), WUSED - wo(6))
         wt[rest, :] = wt[rest, :] - dot(rest5, mine)
 
-    xmate, xnear = 1 - x % 2, x % 2
-
     def inverses6():
         lines = pl.ds(0, R)
         return inv_pair(
-            eye() + (xm[lines, :] + xb[xmate, lines, :]), eye() + (xb[xnear, lines, :] + xb[2, lines, :])
+            eye() + (xm[lines, :] + xb[0, lines, :]), eye() + (xb[1, lines, :] + xb[2, lines, :])
         )
 
     both6 = exchanged(xm, xb, XROWS, xs, prepared5, inverses6, update45)
-    u6[0] = xm[pl.ds(0, 520), :] + xb[xmate, pl.ds(0, 520), :]
-    u6[1] = xb[xnear, pl.ds(0, 520), :] + xb[2, pl.ds(0, 520), :]
+    u6[0] = xm[pl.ds(0, 520), :] + xb[0, pl.ds(0, 520), :]
+    u6[1] = xb[1, pl.ds(0, 520), :] + xb[2, pl.ds(0, 520), :]
     halves = [dot(u6[k, pl.ds(R, 392), :], both6[k]) for k in range(2)]
     for level in range(7, LEVELS + 1):
         n = rows_of(level)
         skip = wo(level) - wo(7)
         there = pl.ds(O[level] - O[6], n)
-        value = (xm[there, :] + xb[xmate, there, :]) + (xb[xnear, there, :] + xb[2, there, :])
+        value = (xm[there, :] + xb[0, there, :]) + (xb[1, there, :] + xb[2, there, :])
         for k in range(2):
             value = value - dot(halves[k][skip:], u6[k, pl.ds(R + skip, R), :], 1, 1)
         s7[pl.ds(O[level] - O[7], n), :] = value
@@ -454,19 +446,17 @@
         ym[pl.ds(264, 136), :] = s7[pl.ds(656, 136), :] - dot(half7, rest7[R : 2 * R], 1, 1)
 
 
-    ymate, ynear = 1 - y % 2, y % 2
-
     def inverses8():
         lines = pl.ds(0, R)
         return inv_pair(
-            eye() + (ym[lines, :] + yb[ymate, lines, :]), eye() + (yb[ynear, lines, :] + yb[2, lines, :])
+            eye() + (ym[lines, :] + yb[0, lines, :]), eye() + (yb[1, lines, :] + yb[2, lines, :])
         )
 
     inverses = exchanged(ym, yb, YROWS, ys, prepared7, inverses8, lambda: None)
     top = pl.ds(0, 264)
-    u8 = [ym[top, :] + yb[ymate, top, :], yb[ynear, top, :] + yb[2, top, :]]
+    u8 = [ym[top, :] + yb[0, top, :], yb[1, top, :] + yb[2, top, :]]
     there = pl.ds(264, 136)
-    s9 = (ym[there, :] + yb[ymate, there, :]) + (yb[ynear, there, :] + yb[2, there, :])
+    s9 = (ym[there, :] + yb[0, there, :]) + (yb[1, there, :] + yb[2, there, :])
     for k in range(2):
         rest = u8[k][R:]
         s9 = s9 - dot(dot(rest, inverses[k]), rest[:R], 1, 1)

time: 192 us -> 181 us (0.943)
  Pallas kernels: 190 us -> 179 us
    pallas_call x1, Pallas kernels: 190 us -> 179 us  [body(): pl.pallas_call(kernel, out_shape=jax.ShapeDtypeStruct((8, LEAF), F32), in...]
where the time goes in v2:
time: 181 us; the launch traced here: 180 us
  Pallas kernels  179 us (99%)
    pallas_call x1, Pallas kernels, body(): pl.pallas_call(kernel, out_shape=jax.ShapeDtypeStruct((8, LEAF), F32), in...  179 us

profile of v2, /device:TPU:1, one launch (start us, length us, event | category | flops | bytes accessed | tf_op | source)
XLA Modules:
  0.0 180.5 jit_solution(6012734254685655532)
XLA Ops:
  0.0 179.2 %tree.1 = f32[8,384]{1,0:T(8,128)} custom-call(s32[511]{0:T(512)} %ranks.1, f32[8,384]{1,0:T(8,128)} %bitcast.3, f32[384,384]{1,0:T(8,128)} %leaves.1, f32[9,384,128]{2,1,0:T(8,128)} %bases.1), custom_call_target="tpu_custom_call" | custom-call | tf_op jit(solution)/shard_map/tree/pallas_call | solution.py:492
  179.2 1.3 copy.6
